TPU v7x, 128 devices: a whole 4x4x4 slice. The times are simulated.
128 devices in a mesh: seq: 16 (over x_lo, y, core), tp: 8 (over x_hi, z).
Axes of the slice: x: 4 (x_hi: 2, x_lo: 2; x = x_hi * 2 + x_lo), y: 4, z: 4, core: 2. Of those that a mesh axis runs over, the one named last changes fastest.
Arguments:
- embeddings: bfloat16 [6144, 4096], P('seq', 'tp'), may hold values from -6 to 6
- span_mask: int32 [6144], P('seq'), may hold values from 0 to 1, as said below
- sentinel_id: int32 [6144], P('seq'), may hold values from 0 to 99, as said below
- sentinel_table: bfloat16 [100, 4096], P(None, 'tp'), may hold values from -6 to 6
- gen_weight: bfloat16 [4096, 240], P(None, 'tp'), may hold values from -0.1875 to 0.1875
- up_weight: bfloat16 [4096, 8192], P(None, 'tp'), may hold values from -0.09375 to 0.09375
- down_weight: bfloat16 [8192, 4096], P('tp'), may hold values from -0.0625 to 0.0625
- cotangent: bfloat16 [6144, 4096], P('seq', 'tp'), may hold values from -0.59765625 to 0.59765625
Outputs:
- layer_output: bfloat16 [6144, 4096], P('seq', 'tp')
- embed_grad: float32 [6144, 4096], P('seq', 'tp')
- table_grad: float32 [100, 4096], P(None, 'tp')
- gen_grad: float32 [4096, 240], P(None, 'tp')
- up_grad: float32 [4096, 8192], P('seq', 'tp')
- down_grad: float32 [8192, 4096], P('tp', 'seq')
Inputs may be any that keep to these rules, and one draw needn't show every extreme that they name: `span_mask`: the tokens fall into aligned blocks of 16; each block holds exactly one span of 1 to 3 consecutive tokens marked 1, the rest 0. `sentinel_id`: all 16 tokens of an aligned block carry the same sentinel id.
All inputs are finite; a program needn't handle non-finite values.
Results may differ from a plain program's by a relative error of at most 0.035.
Values may be sent and summed in bfloat16 or wider, within the bound.
No kernel may reach another device: no remote copies, remote signals or barrier semaphores. Data moves between devices by JAX's collectives and lax.ppermute only.
A program may use at most 192 MiB of HBM per device.

v0:
```python
import jax
import jax.numpy as jnp
from jax import lax
from jax.sharding import PartitionSpec as P

KW = 15
SENT = 100


def with_halo(block, sides, width):
    for axis, dim in sides:
        count = lax.axis_size(axis)
        forward = [(i, i + 1) for i in range(count - 1)]
        backward = [(target, source) for source, target in forward]
        low = lax.ppermute(
            lax.slice_in_dim(block, block.shape[dim] - width, None, axis=dim), axis, forward
        )
        high = lax.ppermute(lax.slice_in_dim(block, 0, width, axis=dim), axis, backward)
        block = jnp.concatenate([low, block, high], axis=dim)
    return block


def gelu_tanh(values):
    return jax.nn.gelu(values, approximate=True)


def body(
    embeddings,
    span_mask,
    sentinel_id,
    sentinel_table,
    gen_weight,
    up_weight,
    down_weight,
    cotangent,
):
    tok_rows, feat_width = embeddings.shape
    head_count = gen_weight.shape[1] // KW
    head_width = feat_width // head_count
    tap_reach = (KW - 1) // 2
    sentinel_codes = jnp.arange(SENT, dtype=jnp.int32)
    onehot = sentinel_id[:, None] == sentinel_codes[None, :]
    picked = jnp.dot(
        onehot.astype(jnp.bfloat16), sentinel_table, preferred_element_type=jnp.float32
    ).astype(jnp.bfloat16)
    masked = span_mask[:, None] == 1
    hidden = jnp.where(masked, picked, embeddings)
    full_hidden = lax.all_gather(hidden, "tp", axis=1, tiled=True)
    logits = jnp.dot(full_hidden, gen_weight, preferred_element_type=jnp.float32)
    exp_logits = jnp.exp(logits.reshape(tok_rows, head_count, KW))
    kernel = exp_logits / jnp.sum(exp_logits, axis=-1, keepdims=True)
    padded = with_halo(hidden, (("seq", 0),), tap_reach)
    padded = padded.reshape(tok_rows + 2 * tap_reach, head_count, head_width)
    conv_sum = jnp.zeros((tok_rows, head_count, head_width), jnp.float32)
    for tap_index in range(KW):
        conv_sum = (
            conv_sum + kernel[:, :, tap_index, None] * padded[tap_index : tap_index + tok_rows]
        )
    act = (hidden.astype(jnp.float32) + conv_sum.reshape(tok_rows, feat_width)).astype(jnp.bfloat16)
    shard_piece = lax.all_gather(act, "tp", axis=1, tiled=True)
    up_rows = up_weight
    pre_sum = jnp.dot(shard_piece, up_rows, preferred_element_type=jnp.float32)
    full_copy = shard_piece
    middle, gelu_back = jax.vjp(gelu_tanh, pre_sum)
    middle = middle.astype(jnp.bfloat16)
    down_cols = down_weight
    ffn_total = lax.psum_scatter(
        lax.dot_general(
            down_cols, middle, (((0,), (1,)), ((), ())), preferred_element_type=jnp.float32
        ).astype(jnp.bfloat16),
        "tp",
        scatter_dimension=0,
        tiled=True,
    ).astype(jnp.float32)
    layer_output = (act.astype(jnp.float32) + ffn_total.T).astype(jnp.bfloat16)
    shard_piece = lax.all_gather(cotangent, "tp", axis=1, tiled=True)
    down_cols = down_weight
    middle_sum = lax.dot_general(
        shard_piece, down_cols, (((1,), (1,)), ((), ())), preferred_element_type=jnp.float32
    )
    block_term = lax.dot_general(
        middle, shard_piece, (((0,), (0,)), ((), ())), preferred_element_type=jnp.float32
    )
    down_term = block_term
    middle_grad, down_term = (middle_sum, down_term)
    down_grad = lax.psum_scatter(
        down_term.astype(jnp.bfloat16), "seq", scatter_dimension=1, tiled=True
    ).astype(jnp.float32)
    pre_grad = gelu_back(middle_grad)[0].astype(jnp.bfloat16)
    up_grad = lax.psum_scatter(
        lax.dot_general(
            full_copy, pre_grad, (((0,), (0,)), ((), ())), preferred_element_type=jnp.float32
        ).astype(jnp.bfloat16),
        "seq",
        scatter_dimension=0,
        tiled=True,
    ).astype(jnp.float32)
    up_rows = up_weight
    act_back = lax.psum_scatter(
        lax.dot_general(
            up_rows, pre_grad, (((1,), (1,)), ((), ())), preferred_element_type=jnp.float32
        ).astype(jnp.bfloat16),
        "tp",
        scatter_dimension=0,
        tiled=True,
    ).astype(jnp.float32)
    act_grad = cotangent.astype(jnp.float32) + act_back.T
    act_three = act_grad.reshape(tok_rows, head_count, head_width)
    kernel_grad = jnp.stack(
        [
            jnp.sum(act_three * padded[tap_index : tap_index + tok_rows], axis=-1)
            for tap_index in range(KW)
        ],
        axis=-1,
    )
    weighted = jnp.sum(kernel * kernel_grad, axis=-1, keepdims=True)
    logit_grad = (
        (kernel * (kernel_grad - weighted)).reshape(tok_rows, head_count * KW).astype(jnp.bfloat16)
    )
    joined = jnp.concatenate([act_grad, kernel.reshape(tok_rows, head_count * KW)], axis=1)
    joined_pad = with_halo(joined.astype(jnp.bfloat16), (("seq", 0),), tap_reach).astype(
        joined.dtype
    )
    grad_pad = joined_pad[:, :feat_width].reshape(tok_rows + 2 * tap_reach, head_count, head_width)
    kernel_pad = joined_pad[:, feat_width:].reshape(tok_rows + 2 * tap_reach, head_count, KW)
    conv_back = jnp.zeros((tok_rows, head_count, head_width), jnp.float32)
    for tap_index in range(KW):
        lower = 2 * tap_reach - tap_index
        conv_back = (
            conv_back
            + kernel_pad[lower : lower + tok_rows, :, tap_index, None]
            * grad_pad[lower : lower + tok_rows]
        )
    gen_part = lax.dot_general(
        full_hidden, logit_grad, (((0,), (0,)), ((), ())), preferred_element_type=jnp.float32
    )
    gen_back = (
        lax.psum_scatter(
            lax.dot_general(
                gen_weight, logit_grad, (((1,), (1,)), ((), ())), preferred_element_type=jnp.float32
            ).astype(jnp.bfloat16),
            "tp",
            scatter_dimension=0,
            tiled=True,
        )
        .astype(jnp.float32)
        .T
    )
    hidden_grad = act_grad + conv_back.reshape(tok_rows, feat_width) + gen_back
    embed_grad = jnp.where(masked, jnp.float32(0.0), hidden_grad)
    table_part = jnp.dot(
        onehot.astype(jnp.float32).T,
        jnp.where(masked, hidden_grad, jnp.float32(0.0)),
        precision=lax.Precision.HIGHEST,
    )
    gen_sum, table_grad = (
        lax.psum(gen_part.astype(jnp.bfloat16), "seq").astype(jnp.float32),
        lax.psum(table_part.astype(jnp.bfloat16), "seq").astype(jnp.float32),
    )
    return (layer_output, embed_grad, table_grad, gen_sum, up_grad, down_grad)


def solution(mesh):
    placed = (
        P("seq", "tp"),
        P("seq"),
        P("seq"),
        P(None, "tp"),
        P(None, "tp"),
        P(None, "tp"),
        P("tp", None),
        P("seq", "tp"),
    )
    return jax.shard_map(
        body,
        mesh=mesh,
        in_specs=placed,
        out_specs=(
            P("seq", "tp"),
            P("seq", "tp"),
            P(None, "tp"),
            P(None, "tp"),
            P("seq", "tp"),
            P("tp", "seq"),
        ),
        check_vma=False,
    )
```

profile of v0, /device:TPU:0, one launch (start us, length us, event | category | flops | bytes accessed | tf_op | source)
XLA Modules:
  0.0 786.1 jit_solution(15642379624280598113)
XLA Ops:
  7.9 2.1 fusion.11
  14.2 63.1 %all-gather.4.cloned.1.call-done = bf16[384,4096]{1,0:T(8,128)(2,1)} async-done(((bf16[384,512]{1,0:T(8,128)(2,1)}), bf16[384,4096]{1,0:T(8,128)(2,1)}) %all-gather.4.cloned.1.call-update) | async-done | bytes 3145744 | tf_op jit(solution)/shard_map/all_gather | solution.py:48
  77.3 2.9 convolution_exponential_fusion
  91.1 2.5 fusion.45
  93.8 47.6 %all-gather.8.cloned.1.call-done = bf16[384,4096]{1,0:T(8,128)(2,1)} async-done(((bf16[384,512]{1,0:T(8,128)(2,1)}), bf16[384,4096]{1,0:T(8,128)(2,1)}) %all-gather.8.cloned.1.call-update) | async-done | bytes 3145744 | tf_op jit(solution)/shard_map/all_gather | solution.py:76
  141.4 6.8 fusion.69
  148.3 57.8 %all-gather.6.cloned.1.call-done = bf16[384,4096]{1,0:T(8,128)(2,1)} async-done(((bf16[384,512]{1,0:T(8,128)(2,1)}), bf16[384,4096]{1,0:T(8,128)(2,1)}) %all-gather.6.cloned.1.call-update) | async-done | bytes 3145744 | tf_op jit(solution)/shard_map/all_gather | solution.py:60
  206.1 9.7 %fusion.10 = (bf16[384,1024]{1,0:T(8,128)(2,1)S(1)}, f32[384,1024]{1,0:T(8,128)}) fusion(f32[384,1024]{1,0:T(8,128)S(1)} %fusion.69, bf16[384,4096]{1,0:T(8,128)(2,1)} %all-gather.6.cloned.1.call-done, bf16[4096,1024]{1,0:T(8,128)(2,1)} %param.13), kind=kOutput, calls=%fused_computation.18 | convolution fusion | flops 3229089792 | bytes 15466496 | tf_op jit(solution)/shard_map/dot_general | solution.py:62
  215.7 10.6 %fusion.2 = bf16[4096,384]{0,1:T(8,128)(2,1)} fusion(bf16[384,1024]{1,0:T(8,128)(2,1)S(1)} %get-tuple-element.62, bf16[4096,1024]{1,0:T(8,128)(2,1)} %param.13), kind=kOutput, calls=%fused_computation.7 | convolution fusion | flops 3222798336 | bytes 12320768 | tf_op jit(solution)/shard_map/dot_general | solution.py:100
  226.9 76.9 %reduce-scatter.8.cloned.1.call-done = bf16[512,384]{0,1:T(8,128)(2,1)} async-done(((bf16[4096,384]{0,1:T(8,128)(2,1)}), bf16[512,384]{0,1:T(8,128)(2,1)}) %reduce-scatter.8.cloned.1.call-update) | async-done | bytes 393232 | tf_op jit(solution)/shard_map/reduce_scatter | solution.py:99
  303.8 3.5 convert_multiply_fusion.16
  321.8 2.7 convert_multiply_fusion.2
  340.6 2.7 fusion.3
  344.7 8.3 %fusion.1 = bf16[4096,384]{0,1:T(8,128)(2,1)} fusion(bf16[1024,4096]{1,0:T(8,128)(2,1)} %param.14, f32[384,1024]{1,0:T(8,128)S(1)} %copy-done.18), kind=kOutput, calls=%fused_computation.6 | convolution fusion | flops 3226337280 | bytes 13107200 | tf_op jit(solution)/shard_map/dot_general | solution.py:68
  387.8 33.8 %reduce-scatter.10.cloned.1.call-done = bf16[512,384]{0,1:T(8,128)(2,1)} async-done(((bf16[4096,384]{0,1:T(8,128)(2,1)}), bf16[512,384]{0,1:T(8,128)(2,1)}) %reduce-scatter.10.cloned.1.call-update) | async-done | bytes 393232 | tf_op jit(solution)/shard_map/reduce_scatter | solution.py:138
  421.6 5.9 broadcast_select_fusion
  429.1 10.3 %convolution_convert_fusion = bf16[1024,4096]{1,0:T(8,128)(2,1)} fusion(bf16[384,4096]{1,0:T(8,128)(2,1)} %all-gather.8.cloned.1.call-done, f32[384,1024]{1,0:T(8,128)} %get-tuple-element.63), kind=kOutput, calls=%fused_computation.1 | convolution fusion | flops 3228958720 | bytes 13107200 | tf_op jit(solution)/shard_map/dot_general | solution.py:81
  441.4 7.9 %convolution_convert_fusion.1 = bf16[4096,1024]{1,0:T(8,128)(2,1)} fusion(bf16[384,4096]{1,0:T(8,128)(2,1)S(1)} %copy-done.17, bf16[384,1024]{1,0:T(8,128)(2,1)} %copy-done.19), kind=kOutput, calls=%fused_computation.2 | convolution fusion | flops 3225419776 | bytes 12320768 | tf_op jit(solution)/shard_map/dot_general | solution.py:91
  449.2 54.4 %reduce-scatter.6.cloned.1.call-done = bf16[512,384]{0,1:T(8,128)(2,1)} async-done(((bf16[4096,384]{0,1:T(8,128)(2,1)}), bf16[512,384]{0,1:T(8,128)(2,1)}) %reduce-scatter.6.cloned.1.call-update) | async-done | bytes 393232 | tf_op jit(solution)/shard_map/reduce_scatter | solution.py:67
  505.5 117.2 %all-reduce.3.cloned.1.call-done = (bf16[100,512]{1,0:T(8,128)(2,1)}, bf16[4096,30]{0,1:T(8,128)(2,1)}) async-done(((bf16[100,512]{1,0:T(8,128)(2,1)}, bf16[4096,30]{0,1:T(8,128)(2,1)}), (bf16[100,512]{1,0:T(8,128)(2,1)}, bf16[4096,30]{0,1:T(8,128)(2,1)})) %all-reduce.3.cloned.1.call-update) | async-done | bytes 348176 | tf_op jit(solution)/shard_map/psum | solution.py:158
  626.1 75.2 %reduce-scatter.14.cloned.1.call-done = bf16[1024,256]{1,0:T(8,128)(2,1)} async-done(((bf16[1024,4096]{1,0:T(8,128)(2,1)}), bf16[1024,256]{1,0:T(8,128)(2,1)}) %reduce-scatter.14.cloned.1.call-update) | async-done | bytes 524304 | tf_op jit(solution)/shard_map/reduce_scatter | solution.py:86
  701.3 2.1 convert_element_type.203
  703.4 73.6 %reduce-scatter.12.cloned.1.call-done = bf16[256,1024]{1,0:T(8,128)(2,1)} async-done(((bf16[4096,1024]{1,0:T(8,128)(2,1)}), bf16[256,1024]{1,0:T(8,128)(2,1)}) %reduce-scatter.12.cloned.1.call-update) | async-done | bytes 524304 | tf_op jit(solution)/shard_map/reduce_scatter | solution.py:90
  777.0 2.1 convert_element_type.201
  (225 shorter events, 91.2 us)
Async XLA Ops:
  7.2 70.2 %copy-start = (bf16[4096,30]{0,1:T(8,128)(2,1)S(1)}, bf16[4096,30]{0,1:T(8,128)(2,1)}, u32[]{:S(2)}) copy-start(bf16[4096,30]{0,1:T(8,128)(2,1)} %param.12) | copy-start | bytes 737284
  7.2 70.2 %all-gather.4.cloned.1.call-start = ((), (), s32[]{:S(2)}) async-start(), calls=%async_computation.5 | async-start | bytes 3538944 | tf_op jit(solution)/shard_map/all_gather | solution.py:48
  10.1 131.3 %all-gather.8.cloned.1.call-start = ((), (), s32[]{:S(2)}) async-start(), calls=%async_computation.8 | async-start | bytes 3538944 | tf_op jit(solution)/shard_map/all_gather | solution.py:76
  10.9 195.2 %all-gather.6.cloned.1.call-start = ((), (), s32[]{:S(2)}) async-start(), calls=%async_computation.6 | async-start | bytes 3538944 | tf_op jit(solution)/shard_map/all_gather | solution.py:60
  11.6 79.0 %collective-permute-start = (bf16[7,512]{1,0:T(8,128)(2,1)S(1)}, bf16[7,512]{1,0:T(8,128)(2,1)S(1)}, u32[]{:S(2)}, u32[]{:S(2)}) collective-permute-start(bf16[7,512]{1,0:T(8,128)(2,1)S(1)} %get-tuple-element.28), channel_id=1, source_target_pairs={{0,8},{8,16},{16,24},{24,32},{32,40},{40,48},{48,56},{56,64},{64,7... | collective-permute-start | bytes 21512 | tf_op jit(solution)/shard_map/ppermute | solution.py:15
  12.9 77.7 %collective-permute-start.1 = (bf16[7,512]{1,0:T(8,128)(2,1)S(1)}, bf16[7,512]{1,0:T(8,128)(2,1)S(1)}, u32[]{:S(2)}, u32[]{:S(2)}) collective-permute-start(bf16[7,512]{1,0:T(8,128)(2,1)S(1)} %get-tuple-element.29), channel_id=1, source_target_pairs={{8,0},{16,8},{24,16},{32,24},{40,32},{48,40},{56,48},{64,56},{72,6... | collective-permute-start | bytes 21512 | tf_op jit(solution)/shard_map/ppermute | solution.py:18
  93.6 210.2 %reduce-scatter.8.cloned.1.call-start = ((), (), s32[]{:S(2)}) async-start(), calls=%async_computation.9 | async-start | bytes 3538944 | tf_op jit(solution)/shard_map/reduce_scatter | solution.py:99
  215.7 10.6 %copy-start.19 = (bf16[384,1024]{1,0:T(8,128)(2,1)}, bf16[384,1024]{1,0:T(8,128)(2,1)S(1)}, u32[]{:S(2)}) copy-start(bf16[384,1024]{1,0:T(8,128)(2,1)S(1)} %get-tuple-element.62) | copy-start | bytes 2359300
  226.4 77.4 %copy-start.4 = (bf16[384,512]{1,0:T(8,128)(2,1)S(1)}, bf16[384,512]{1,0:T(8,128)(2,1)}, u32[]{:S(2)}) copy-start(bf16[384,512]{1,0:T(8,128)(2,1)} %param.15) | copy-start | bytes 1179652
  226.4 195.2 %reduce-scatter.10.cloned.1.call-start = ((), (), s32[]{:S(2)}) async-start(), calls=%async_computation.10 | async-start | bytes 3538944 | tf_op jit(solution)/shard_map/reduce_scatter | solution.py:138
  343.3 160.3 %reduce-scatter.6.cloned.1.call-start = ((), (), s32[]{:S(2)}) async-start(), calls=%async_computation.7 | async-start | bytes 3538944 | tf_op jit(solution)/shard_map/reduce_scatter | solution.py:67
  353.0 4.0 copy-start.2
  353.0 269.6 %all-reduce.3.cloned.1.call-start = ((), (), s32[]{:S(2)}) async-start(), calls=%async_computation.13 | async-start | bytes 737280 | tf_op jit(solution)/shard_map/psum | solution.py:158
  354.1 4.3 collective-permute-start.2
  355.4 5.0 copy-start.9
  355.4 4.9 collective-permute-start.3
  386.4 35.2 %copy-start.5 = (bf16[384,512]{1,0:T(8,128)(2,1)S(1)}, bf16[384,512]{1,0:T(8,128)(2,1)}, u32[]{:S(2)}) copy-start(bf16[384,512]{1,0:T(8,128)(2,1)} %param.15) | copy-start | bytes 1179652
  386.4 35.2 %copy-start.8 = (bf16[512,384]{0,1:T(8,128)(2,1)S(1)}, bf16[512,384]{0,1:T(8,128)(2,1)}, u32[]{:S(2)}) copy-start(bf16[512,384]{0,1:T(8,128)(2,1)} %reduce-scatter.8.cloned.1.call-done) | copy-start | bytes 1179652
  421.6 5.9 copy-start.16
  428.8 272.5 %reduce-scatter.14.cloned.1.call-start = ((), (), s32[]{:S(2)}) async-start(), calls=%async_computation.12 | async-start | bytes 8912896 | tf_op jit(solution)/shard_map/reduce_scatter | solution.py:86
  439.4 1.9 copy-start.17
  439.5 337.6 %reduce-scatter.12.cloned.1.call-start = ((), (), s32[]{:S(2)}) async-start(), calls=%async_computation.11 | async-start | bytes 8912896 | tf_op jit(solution)/shard_map/reduce_scatter | solution.py:90
  449.2 54.4 %copy-start.6 = (bf16[384,512]{1,0:T(8,128)(2,1)S(1)}, bf16[384,512]{1,0:T(8,128)(2,1)}, u32[]{:S(2)}) copy-start(bf16[384,512]{1,0:T(8,128)(2,1)} %fusion.45) | copy-start | bytes 1179652
  624.2 154.9 %copy-start.1 = (bf16[4096,30]{0,1:T(8,128)(2,1)S(1)}, bf16[4096,30]{0,1:T(8,128)(2,1)}, u32[]{:S(2)}) copy-start(bf16[4096,30]{0,1:T(8,128)(2,1)} %param.12) | copy-start | bytes 737284
  (9 other events, 12.1 us)
Sparse Core Ops, SparseCore 0:
  10.8 66.5 all-gather.3
  79.5 61.8 all-gather.7
  144.2 61.8 all-gather.5
  226.5 77.2 reduce-scatter.7
  343.4 78.1 reduce-scatter.9
  425.3 78.2 reduce-scatter.5
  506.7 115.8 all-reduce.2
  625.2 76.0 reduce-scatter.13
  703.9 73.1 reduce-scatter.11
where the time goes:
time: 795 us; the launch traced here: 786 us
  waiting for transfers between devices  602 us (76%)
  local copies, waits for them, and re-layouts  64.7 us (8%)
  matrix products  64 us (8%)
  other arithmetic  33.2 us (4%)
  between operations  15.1 us (2%)
    psum x1, waiting for transfers between devices, body(): lax.psum(table_part.astype(jnp.bfloat16), 'seq').astype(jnp.float32)  117 us
    reduce_scatter x1, waiting for transfers between devices, body(): lax.psum_scatter(lax.dot_general(up_rows, pre_grad, (((1,), (1,)), ((), (...  76.9 us
    reduce_scatter x1, waiting for transfers between devices, body(): lax.psum_scatter(down_term.astype(jnp.bfloat16), 'seq', scatter_dimension...  75.2 us
    reduce_scatter x1, waiting for transfers between devices, body(): lax.psum_scatter(lax.dot_general(full_copy, pre_grad, (((0,), (0,)), ((),...  73.6 us
    all_gather x1, waiting for transfers between devices, body(): full_hidden = lax.all_gather(hidden, 'tp', axis=1, tiled=True)  63.1 us
    all_gather x1, waiting for transfers between devices, body(): shard_piece = lax.all_gather(act, 'tp', axis=1, tiled=True)  57.8 us
    reduce_scatter x1, waiting for transfers between devices, body(): lax.psum_scatter(lax.dot_general(down_cols, middle, (((0,), (1,)), ((), (...  54.4 us
    all_gather x1, waiting for transfers between devices, body(): shard_piece = lax.all_gather(cotangent, 'tp', axis=1, tiled=True)  47.6 us
  transfers between devices with their start and end apart: 13, of which 10 were waited for; matrix products, arithmetic and copies ran while one was open for 12% of the time, Pallas kernels for 0%

commit v1 on v0

--- a/solution.py
+++ b/solution.py
@@ -155,7 +155,7 @@
     )
     gen_sum, table_grad = (
         lax.psum(gen_part.astype(jnp.bfloat16), "seq").astype(jnp.float32),
-        lax.psum(table_part.astype(jnp.bfloat16), "seq").astype(jnp.float32),
+        jnp.sum(lax.all_gather(table_part.astype(jnp.bfloat16), "seq"), axis=0).astype(jnp.float32),
     )
     return (layer_output, embed_grad, table_grad, gen_sum, up_grad, down_grad)
 

time: 795 us -> 829 us (1.043)
  waiting for transfers between devices: 602 us -> 635 us
    all_gather x0 -> x1, waiting for transfers between devices: none -> 35.2 us  [body(): lax.all_gather(table_part.astype(jnp.bfloat16), 'seq')]
    unnamed x70 -> x68, local copies, waits for them, and re-layouts: 18.1 us -> 18 us
  transfers between devices with their start and end apart: 13 -> 14, of which waited for: 10 -> 11; matrix products, arithmetic and copies ran while one was open for 12% -> 12% of each run, Pallas kernels for 0% -> 0%
where the time goes in v1:
time: 829 us; the launch traced here: 821 us
  waiting for transfers between devices  635 us (77%)
  local copies, waits for them, and re-layouts  64.6 us (8%)
  matrix products  63.9 us (8%)
  other arithmetic  34.9 us (4%)
  between operations  15.4 us (2%)
    psum x1, waiting for transfers between devices, body(): lax.psum(gen_part.astype(jnp.bfloat16), 'seq').astype(jnp.float32)  116 us
    reduce_scatter x1, waiting for transfers between devices, body(): lax.psum_scatter(lax.dot_general(up_rows, pre_grad, (((1,), (1,)), ((), (...  76.9 us
    reduce_scatter x1, waiting for transfers between devices, body(): lax.psum_scatter(down_term.astype(jnp.bfloat16), 'seq', scatter_dimension...  74.8 us
    reduce_scatter x1, waiting for transfers between devices, body(): lax.psum_scatter(lax.dot_general(full_copy, pre_grad, (((0,), (0,)), ((),...  73.6 us
    all_gather x1, waiting for transfers between devices, body(): full_hidden = lax.all_gather(hidden, 'tp', axis=1, tiled=True)  63.1 us
    all_gather x1, waiting for transfers between devices, body(): shard_piece = lax.all_gather(act, 'tp', axis=1, tiled=True)  57.8 us
    reduce_scatter x1, waiting for transfers between devices, body(): lax.psum_scatter(lax.dot_general(down_cols, middle, (((0,), (1,)), ((), (...  54.3 us
    all_gather x1, waiting for transfers between devices, body(): shard_piece = lax.all_gather(cotangent, 'tp', axis=1, tiled=True)  47.6 us
  transfers between devices with their start and end apart: 14, of which 11 were waited for; matrix products, arithmetic and copies ran while one was open for 12% of the time, Pallas kernels for 0%

profile of v1, /device:TPU:0, one launch (start us, length us, event | category | flops | bytes accessed | tf_op | source)
XLA Modules:
  0.0 820.5 jit_solution(16154581846238026128)
XLA Ops:
  7.9 2.1 fusion.11
  14.2 63.1 %all-gather.7.cloned.1.call-done = bf16[384,4096]{1,0:T(8,128)(2,1)} async-done(((bf16[384,512]{1,0:T(8,128)(2,1)}), bf16[384,4096]{1,0:T(8,128)(2,1)}) %all-gather.7.cloned.1.call-update) | async-done | bytes 3145744 | tf_op jit(solution)/shard_map/all_gather | solution.py:48
  77.3 2.9 convolution_exponential_fusion
  91.1 2.5 fusion.46
  93.8 47.6 %all-gather.11.cloned.1.call-done = bf16[384,4096]{1,0:T(8,128)(2,1)} async-done(((bf16[384,512]{1,0:T(8,128)(2,1)}), bf16[384,4096]{1,0:T(8,128)(2,1)}) %all-gather.11.cloned.1.call-update) | async-done | bytes 3145744 | tf_op jit(solution)/shard_map/all_gather | solution.py:76
  141.4 6.8 fusion.70
  148.3 57.8 %all-gather.9.cloned.1.call-done = bf16[384,4096]{1,0:T(8,128)(2,1)} async-done(((bf16[384,512]{1,0:T(8,128)(2,1)}), bf16[384,4096]{1,0:T(8,128)(2,1)}) %all-gather.9.cloned.1.call-update) | async-done | bytes 3145744 | tf_op jit(solution)/shard_map/all_gather | solution.py:60
  206.1 9.7 %fusion.10 = (bf16[384,1024]{1,0:T(8,128)(2,1)S(1)}, f32[384,1024]{1,0:T(8,128)}) fusion(f32[384,1024]{1,0:T(8,128)S(1)} %fusion.70, bf16[384,4096]{1,0:T(8,128)(2,1)} %all-gather.9.cloned.1.call-done, bf16[4096,1024]{1,0:T(8,128)(2,1)} %param.13), kind=kOutput, calls=%fused_computation.18 | convolution fusion | flops 3229089792 | bytes 15466496 | tf_op jit(solution)/shard_map/dot_general | solution.py:62
  215.7 10.6 %fusion.2 = bf16[4096,384]{0,1:T(8,128)(2,1)} fusion(bf16[384,1024]{1,0:T(8,128)(2,1)S(1)} %get-tuple-element.60, bf16[4096,1024]{1,0:T(8,128)(2,1)} %param.13), kind=kOutput, calls=%fused_computation.7 | convolution fusion | flops 3222798336 | bytes 12320768 | tf_op jit(solution)/shard_map/dot_general | solution.py:100
  226.9 76.9 %reduce-scatter.8.cloned.1.call-done = bf16[512,384]{0,1:T(8,128)(2,1)} async-done(((bf16[4096,384]{0,1:T(8,128)(2,1)}), bf16[512,384]{0,1:T(8,128)(2,1)}) %reduce-scatter.8.cloned.1.call-update) | async-done | bytes 393232 | tf_op jit(solution)/shard_map/reduce_scatter | solution.py:99
  303.8 3.5 convert_multiply_fusion.16
  321.8 2.7 convert_multiply_fusion.2
  340.5 2.7 fusion.3
  344.6 8.3 %fusion.1 = bf16[4096,384]{0,1:T(8,128)(2,1)} fusion(bf16[1024,4096]{1,0:T(8,128)(2,1)} %param.14, f32[384,1024]{1,0:T(8,128)S(1)} %copy-done.17), kind=kOutput, calls=%fused_computation.6 | convolution fusion | flops 3226337280 | bytes 13107200 | tf_op jit(solution)/shard_map/dot_general | solution.py:68
  388.6 33.1 %reduce-scatter.10.cloned.1.call-done = bf16[512,384]{0,1:T(8,128)(2,1)} async-done(((bf16[4096,384]{0,1:T(8,128)(2,1)}), bf16[512,384]{0,1:T(8,128)(2,1)}) %reduce-scatter.10.cloned.1.call-update) | async-done | bytes 393232 | tf_op jit(solution)/shard_map/reduce_scatter | solution.py:138
  421.6 5.9 broadcast_select_fusion
  429.1 10.3 %convolution_convert_fusion = bf16[1024,4096]{1,0:T(8,128)(2,1)} fusion(bf16[384,4096]{1,0:T(8,128)(2,1)} %all-gather.11.cloned.1.call-done, f32[384,1024]{1,0:T(8,128)} %get-tuple-element.61), kind=kOutput, calls=%fused_computation.1 | convolution fusion | flops 3228958720 | bytes 13107200 | tf_op jit(solution)/shard_map/dot_general | solution.py:81
  441.4 7.9 convolution_convert_fusion.1
  449.2 54.3 %reduce-scatter.6.cloned.1.call-done = bf16[512,384]{0,1:T(8,128)(2,1)} async-done(((bf16[4096,384]{0,1:T(8,128)(2,1)}), bf16[512,384]{0,1:T(8,128)(2,1)}) %reduce-scatter.6.cloned.1.call-update) | async-done | bytes 393232 | tf_op jit(solution)/shard_map/reduce_scatter | solution.py:67
  505.4 115.8 %all-reduce.2.cloned.1.call-done = bf16[4096,30]{0,1:T(8,128)(2,1)} async-done(((bf16[4096,30]{0,1:T(8,128)(2,1)}), bf16[4096,30]{0,1:T(8,128)(2,1)}) %all-reduce.2.cloned.1.call-update) | async-done | bytes 245776 | tf_op jit(solution)/shard_map/psum | solution.py:157
  623.0 35.2 %all-gather.13.cloned.1.call-done = bf16[16,100,512]{2,1,0:T(8,128)(2,1)} async-done(((bf16[1,100,512]{2,1,0:T(8,128)(2,1)}), bf16[16,100,512]{2,1,0:T(8,128)(2,1)}) %all-gather.13.cloned.1.call-update) | async-done | bytes 1638416 | tf_op jit(solution)/shard_map/all_gather | solution.py:158
  660.6 74.8 %reduce-scatter.14.cloned.1.call-done = bf16[1024,256]{1,0:T(8,128)(2,1)} async-done(((bf16[1024,4096]{1,0:T(8,128)(2,1)}), bf16[1024,256]{1,0:T(8,128)(2,1)}) %reduce-scatter.14.cloned.1.call-update) | async-done | bytes 524304 | tf_op jit(solution)/shard_map/reduce_scatter | solution.py:86
  737.5 73.6 %reduce-scatter.12.cloned.1.call-done = bf16[256,1024]{1,0:T(8,128)(2,1)} async-done(((bf16[4096,1024]{1,0:T(8,128)(2,1)}), bf16[256,1024]{1,0:T(8,128)(2,1)}) %reduce-scatter.12.cloned.1.call-update) | async-done | bytes 524304 | tf_op jit(solution)/shard_map/reduce_scatter | solution.py:90
  811.1 2.1 convert_element_type.203
  (227 shorter events, 94.8 us)
Async XLA Ops:
  7.2 70.2 %copy-start = (bf16[4096,30]{0,1:T(8,128)(2,1)S(1)}, bf16[4096,30]{0,1:T(8,128)(2,1)}, u32[]{:S(2)}) copy-start(bf16[4096,30]{0,1:T(8,128)(2,1)} %param.12) | copy-start | bytes 737284
  7.2 70.2 %all-gather.7.cloned.1.call-start = ((), (), s32[]{:S(2)}) async-start(), calls=%async_computation.5 | async-start | bytes 3538944 | tf_op jit(solution)/shard_map/all_gather | solution.py:48
  10.1 131.3 %all-gather.11.cloned.1.call-start = ((), (), s32[]{:S(2)}) async-start(), calls=%async_computation.8 | async-start | bytes 3538944 | tf_op jit(solution)/shard_map/all_gather | solution.py:76
  10.9 195.2 %all-gather.9.cloned.1.call-start = ((), (), s32[]{:S(2)}) async-start(), calls=%async_computation.6 | async-start | bytes 3538944 | tf_op jit(solution)/shard_map/all_gather | solution.py:60
  11.6 79.0 %collective-permute-start = (bf16[7,512]{1,0:T(8,128)(2,1)S(1)}, bf16[7,512]{1,0:T(8,128)(2,1)S(1)}, u32[]{:S(2)}, u32[]{:S(2)}) collective-permute-start(bf16[7,512]{1,0:T(8,128)(2,1)S(1)} %get-tuple-element.26), channel_id=1, source_target_pairs={{0,8},{8,16},{16,24},{24,32},{32,40},{40,48},{48,56},{56,64},{64,7... | collective-permute-start | bytes 21512 | tf_op jit(solution)/shard_map/ppermute | solution.py:15
  12.9 77.7 %collective-permute-start.1 = (bf16[7,512]{1,0:T(8,128)(2,1)S(1)}, bf16[7,512]{1,0:T(8,128)(2,1)S(1)}, u32[]{:S(2)}, u32[]{:S(2)}) collective-permute-start(bf16[7,512]{1,0:T(8,128)(2,1)S(1)} %get-tuple-element.27), channel_id=1, source_target_pairs={{8,0},{16,8},{24,16},{32,24},{40,32},{48,40},{56,48},{64,56},{72,6... | collective-permute-start | bytes 21512 | tf_op jit(solution)/shard_map/ppermute | solution.py:18
  93.6 210.2 %reduce-scatter.8.cloned.1.call-start = ((), (), s32[]{:S(2)}) async-start(), calls=%async_computation.9 | async-start | bytes 3538944 | tf_op jit(solution)/shard_map/reduce_scatter | solution.py:99
  215.7 10.6 %copy-start.18 = (bf16[384,1024]{1,0:T(8,128)(2,1)}, bf16[384,1024]{1,0:T(8,128)(2,1)S(1)}, u32[]{:S(2)}) copy-start(bf16[384,1024]{1,0:T(8,128)(2,1)S(1)} %get-tuple-element.60) | copy-start | bytes 2359300
  226.4 77.4 %copy-start.4 = (bf16[384,512]{1,0:T(8,128)(2,1)S(1)}, bf16[384,512]{1,0:T(8,128)(2,1)}, u32[]{:S(2)}) copy-start(bf16[384,512]{1,0:T(8,128)(2,1)} %param.15) | copy-start | bytes 1179652
  226.4 195.2 %reduce-scatter.10.cloned.1.call-start = ((), (), s32[]{:S(2)}) async-start(), calls=%async_computation.10 | async-start | bytes 3538944 | tf_op jit(solution)/shard_map/reduce_scatter | solution.py:138
  343.2 160.3 %reduce-scatter.6.cloned.1.call-start = ((), (), s32[]{:S(2)}) async-start(), calls=%async_computation.7 | async-start | bytes 3538944 | tf_op jit(solution)/shard_map/reduce_scatter | solution.py:67
  352.9 3.7 copy-start.2
  352.9 268.3 %all-reduce.2.cloned.1.call-start = ((), (), s32[]{:S(2)}) async-start(), calls=%async_computation.11 | async-start | bytes 524288 | tf_op jit(solution)/shard_map/psum | solution.py:157
  354.0 4.2 collective-permute-start.2
  355.3 4.8 collective-permute-start.3
  357.9 300.2 %all-gather.13.cloned.1.call-start = ((), (), s32[]{:S(2)}) async-start(), calls=%async_computation.14 | async-start | bytes 1810432 | tf_op jit(solution)/shard_map/all_gather | solution.py:158
  387.1 34.5 %copy-start.5 = (bf16[384,512]{1,0:T(8,128)(2,1)S(1)}, bf16[384,512]{1,0:T(8,128)(2,1)}, u32[]{:S(2)}) copy-start(bf16[384,512]{1,0:T(8,128)(2,1)} %param.15) | copy-start | bytes 1179652
  387.1 34.5 %copy-start.8 = (bf16[512,384]{0,1:T(8,128)(2,1)S(1)}, bf16[512,384]{0,1:T(8,128)(2,1)}, u32[]{:S(2)}) copy-start(bf16[512,384]{0,1:T(8,128)(2,1)} %reduce-scatter.8.cloned.1.call-done) | copy-start | bytes 1179652
  421.6 5.9 copy-start.15
  428.8 306.6 %reduce-scatter.14.cloned.1.call-start = ((), (), s32[]{:S(2)}) async-start(), calls=%async_computation.13 | async-start | bytes 8912896 | tf_op jit(solution)/shard_map/reduce_scatter | solution.py:86
  439.4 1.9 copy-start.16
  439.5 371.6 %reduce-scatter.12.cloned.1.call-start = ((), (), s32[]{:S(2)}) async-start(), calls=%async_computation.12 | async-start | bytes 8912896 | tf_op jit(solution)/shard_map/reduce_scatter | solution.py:90
  449.2 54.3 %copy-start.6 = (bf16[384,512]{1,0:T(8,128)(2,1)S(1)}, bf16[384,512]{1,0:T(8,128)(2,1)}, u32[]{:S(2)}) copy-start(bf16[384,512]{1,0:T(8,128)(2,1)} %fusion.46) | copy-start | bytes 1179652
  659.9 153.3 %copy-start.1 = (bf16[4096,30]{0,1:T(8,128)(2,1)S(1)}, bf16[4096,30]{0,1:T(8,128)(2,1)}, u32[]{:S(2)}) copy-start(bf16[4096,30]{0,1:T(8,128)(2,1)} %param.12) | copy-start | bytes 737284
  (9 other events, 12.1 us)
Sparse Core Ops, SparseCore 0:
  10.8 66.5 all-gather.6
  79.5 61.8 all-gather.10
  144.2 61.8 all-gather.8
  226.5 77.2 reduce-scatter.7
  343.3 78.2 reduce-scatter.9
  425.3 78.1 reduce-scatter.5
  506.0 115.1 all-reduce.1
  623.6 34.5 all-gather.12
  660.7 74.6 reduce-scatter.13
  737.8 73.2 reduce-scatter.11
